TPU v7x, 128 devices: a whole 4x4x4 slice. The times are simulated.
128 devices in a mesh: vid: 4 (over z_lo, core), tm: 32 (over x, z_hi, y).
Axes of the slice: x: 4, y: 4, z: 4 (z_hi: 2, z_lo: 2; z = z_hi * 2 + z_lo), core: 2. Of those that a mesh axis runs over, the one named last changes fastest.
Arguments:
- video: bfloat16 [4, 8192, 2048], P('vid', 'tm'), may hold values from -6 to 6
- norm_gain: bfloat16 [2048], replicated, may hold values from 0.099609375 to 1.8984375
- query_weight: bfloat16 [2048, 1024], P(('vid', 'tm')), may hold values from -6 to 6
- key_weight: bfloat16 [2048, 1024], P(('vid', 'tm')), may hold values from -0.125 to 0.125
- value_weight: bfloat16 [2048, 1024], P(('vid', 'tm')), may hold values from -0.125 to 0.125
- key_kernel: bfloat16 [27, 1024], replicated, may hold values from -1.25 to 1.25
- value_kernel: bfloat16 [27, 1024], replicated, may hold values from -1.25 to 1.25
- out_weight: bfloat16 [1024, 2048], P(('vid', 'tm')), may hold values from -0.1875 to 0.1875
- frames_valid: int32 [4], replicated, may hold values from 64 to 128, as said below
Outputs:
- attended: bfloat16 [4, 8192, 2048], P('vid', 'tm')
Inputs may be any that keep to these rules, and one draw needn't show every extreme that they name: `frames_valid`: one video has all 128 frames valid.
All inputs are finite; a program needn't handle non-finite values.
Results may differ from a plain program's by a relative error of at most 0.006.
The roundings to bfloat16 on the way count: a program that leaves them out, or rounds other values in their place, can miss the bound.
Values may be sent and summed in bfloat16 or wider, within the bound.
A program may use at most 64 MiB of HBM per device.

v0:
```python
import math

import jax
import jax.numpy as jnp
from jax import lax
from jax.sharding import PartitionSpec as P

HEADS = 8
HD = 128
SIDE = 8


def shifted(value, axis, steps):
    count = lax.axis_size(axis)
    leading, last = (max(0, -steps), min(count, count - steps))
    return lax.ppermute(value, axis, [(source, source + steps) for source in range(leading, last)])


def normalize(rows, gain):
    values = rows.astype(jnp.float32)
    center = jnp.mean(values, axis=-1, keepdims=True)
    spread = jnp.mean((values - center) ** 2, axis=-1, keepdims=True)
    return ((values - center) * lax.rsqrt(spread + 1e-06) * gain.astype(jnp.float32)).astype(
        jnp.bfloat16
    )


def pool_frames(frames, previous, kernel):
    count, side = (frames.shape[0], frames.shape[1])
    width = frames.shape[3]
    half_f, half_s = (count // 2, side // 2)
    stacked = jnp.concatenate([previous[None], frames], axis=0).astype(jnp.float32)
    padded = jnp.pad(stacked, ((0, 0), (1, 1), (1, 1), (0, 0)))
    taps = kernel.astype(jnp.float32)
    total = jnp.zeros((half_f, half_s, half_s, width), jnp.float32)
    for step_t in range(3):
        for step_h in range(3):
            for step_w in range(3):
                piece = padded[
                    2 - step_t : 2 - step_t + 2 * half_f - 1 : 2,
                    step_h : step_h + 2 * half_s - 1 : 2,
                    step_w : step_w + 2 * half_s - 1 : 2,
                ]
                total = total + piece * taps[9 * step_t + 3 * step_h + step_w]
    grouped = total.reshape(half_f * half_s * half_s, HEADS, width // HEADS)
    center = jnp.mean(grouped, axis=-1, keepdims=True)
    spread = jnp.mean((grouped - center) ** 2, axis=-1, keepdims=True)
    normed = (grouped - center) * lax.rsqrt(spread + 1e-06)
    return normed.reshape(half_f * half_s * half_s, width).astype(jnp.bfloat16)


def absorb(state, queries, keys, values, allowed):
    top, total, accum = state
    count = keys.shape[0]
    keys3 = keys.reshape(count, HEADS, HD)
    values3 = values.reshape(count, HEADS, HD).astype(jnp.float32)
    scores = jnp.einsum("qhd,khd->hqk", queries, keys3, preferred_element_type=jnp.float32) * (
        1.0 / math.sqrt(HD)
    )
    scores = jnp.where(allowed, scores, -1e30)
    new_top = jnp.maximum(top, jnp.max(scores, axis=-1))
    factor = jnp.exp(top - new_top)
    weights = jnp.exp(scores - new_top[..., None])
    total = total * factor + jnp.sum(weights, axis=-1)
    accum = accum * factor[..., None] + jnp.einsum(
        "hqk,khd->hqd", weights, values3, precision=lax.Precision.HIGHEST
    )
    return (new_top, total, accum)


def on_device(
    video,
    norm_gain,
    query_weight,
    key_weight,
    value_weight,
    key_kernel,
    value_kernel,
    out_weight,
    frames_valid,
):
    tokens = video[0]
    rows = tokens.shape[0]
    spatial = SIDE * SIDE
    width = query_weight.shape[1]
    count_f = rows // spatial
    normed = normalize(tokens, norm_gain)

    def add_rows(piece):
        return jnp.dot(normed, piece, preferred_element_type=jnp.float32)

    query = add_rows(lax.all_gather(query_weight, ("vid", "tm"), axis=0, tiled=True))
    key = add_rows(lax.all_gather(key_weight, ("vid", "tm"), axis=0, tiled=True))
    value = add_rows(lax.all_gather(value_weight, ("vid", "tm"), axis=0, tiled=True))
    query = query.astype(jnp.bfloat16)
    key = key.astype(jnp.bfloat16)
    value = value.astype(jnp.bfloat16)
    limit = frames_valid[lax.axis_index("vid")]
    block = lax.axis_index("tm")
    frame = jnp.arange(rows, dtype=jnp.int32) // spatial + block * count_f
    valid = frame < limit
    zero = jnp.zeros_like(key)
    masked_key = jnp.where(valid[:, None], key, zero).reshape(count_f, SIDE, SIDE, width)
    masked_value = jnp.where(valid[:, None], value, zero).reshape(count_f, SIDE, SIDE, width)
    prev_key, prev_value = shifted((masked_key[-1], masked_value[-1]), "tm", 1)
    pooled_key = pool_frames(masked_key, prev_key, key_kernel)
    pooled_value = pool_frames(masked_value, prev_value, value_kernel)
    mem_dev = pooled_key.shape[0]
    queries = query.reshape(rows, HEADS, HD)
    local_ok = (frame[None, :] <= frame[:, None]) & valid[None, :]
    state = (
        jnp.full((HEADS, rows), -1e30, jnp.float32),
        jnp.zeros((HEADS, rows), jnp.float32),
        jnp.zeros((HEADS, rows, HD), jnp.float32),
    )
    state = absorb(state, queries, key, value, local_ok[None])
    pieces = (
        lax.all_gather(pooled_key, "tm", axis=0, tiled=True),
        lax.all_gather(pooled_value, "tm", axis=0, tiled=True),
    )
    count = pieces[0].shape[0]
    index = jnp.arange(count, dtype=jnp.int32)
    mem_frame = index // (spatial // 4)
    allowed = (2 * mem_frame < limit) & (index // mem_dev <= block)
    state = absorb(state, queries, pieces[0], pieces[1], allowed[None, None, :])
    top, total, accum = state
    mixed = accum / total[..., None]
    heads = jnp.transpose(mixed, (1, 0, 2)).reshape(rows, width).astype(jnp.bfloat16)
    result = jnp.dot(
        heads,
        lax.all_gather(out_weight, ("vid", "tm"), axis=0, tiled=True),
        preferred_element_type=jnp.float32,
    )
    result = jnp.where(valid[:, None], result, 0.0).astype(jnp.bfloat16)
    return result[None]


def solution(mesh):
    in_specs = (
        P("vid", "tm", None),
        P(),
        P(("vid", "tm"), None),
        P(("vid", "tm"), None),
        P(("vid", "tm"), None),
        P(),
        P(),
        P(("vid", "tm"), None),
        P(),
    )
    out_specs = P("vid", "tm", None)
    return jax.shard_map(
        on_device, mesh=mesh, in_specs=in_specs, out_specs=out_specs, check_vma=False
    )
```

profile of v0, /device:TPU:1, one launch (start us, length us, event | category | flops | bytes accessed | tf_op | source)
XLA Modules:
  0.0 1395.0 jit_solution(7983573533030563817)
XLA Ops:
  15.2 301.9 %all-gather.9.cloned.1.call-done = bf16[2048,1024]{1,0:T(8,128)(2,1)} async-done(((bf16[16,1024]{1,0:T(8,128)(2,1)}), bf16[2048,1024]{1,0:T(8,128)(2,1)}) %all-gather.9.cloned.1.call-update) | async-done | bytes 4194320 | tf_op jit(solution)/shard_map/all_gather | solution.py:93
  317.1 3.5 convolution_convert_fusion.1
  320.6 304.1 %all-gather.11.cloned.1.call-done = bf16[2048,1024]{1,0:T(8,128)(2,1)} async-done(((bf16[16,1024]{1,0:T(8,128)(2,1)}), bf16[2048,1024]{1,0:T(8,128)(2,1)}) %all-gather.11.cloned.1.call-update) | async-done | bytes 4194320 | tf_op jit(solution)/shard_map/all_gather | solution.py:94
  624.8 4.3 broadcast_select_fusion
  629.1 2.7 collective-permute-start.1
  635.8 2.5 slice.392
  640.8 2.5 slice.396
  643.3 2.5 slice.398
  648.3 2.5 slice.402
  650.8 2.6 slice.404
  655.9 2.5 slice.408
  658.4 2.5 slice.410
  663.4 2.5 slice.414
  665.9 2.5 slice.416
  670.9 2.5 slice.420
  673.5 2.5 slice.422
  681.0 2.5 slice.428
  686.0 2.5 slice.432
  688.5 2.5 slice.434
  693.5 2.5 slice.438
  696.0 2.5 slice.440
  698.6 2.9 multiply_add_fusion
  704.4 3.8 collective-permute-start
  713.0 2.5 slice.337
  720.5 2.5 slice.343
  725.6 2.5 slice.347
  728.1 2.5 slice.349
  733.1 2.5 slice.353
  735.6 2.5 slice.355
  740.6 2.5 slice.359
  743.1 2.5 slice.361
  748.2 2.5 slice.365
  750.7 2.5 slice.367
  758.2 2.5 slice.373
  763.2 2.5 slice.377
  765.7 2.5 slice.379
  770.7 2.5 slice.383
  773.2 2.6 slice.385
  775.8 2.9 multiply_add_fusion.1
  781.7 151.7 %all-gather.7.cloned.1.call-done = bf16[2048,1024]{1,0:T(8,128)(2,1)} async-done(((bf16[16,1024]{1,0:T(8,128)(2,1)}), bf16[2048,1024]{1,0:T(8,128)(2,1)}) %all-gather.7.cloned.1.call-update) | async-done | bytes 4194320 | tf_op jit(solution)/shard_map/all_gather | solution.py:92
  933.5 3.5 fusion.29
  938.8 67.7 %all-gather.15.cloned.1.call-done = bf16[1024,1024]{1,0:T(8,128)(2,1)} async-done(((bf16[32,1024]{1,0:T(8,128)(2,1)}), bf16[1024,1024]{1,0:T(8,128)(2,1)}) %all-gather.15.cloned.1.call-update) | async-done | bytes 2097168 | tf_op jit(solution)/shard_map/all_gather | solution.py:119
  1006.5 4.0 copy.46
  1010.5 67.6 %all-gather.13.cloned.1.call-done = bf16[1024,1024]{1,0:T(8,128)(2,1)} async-done(((bf16[32,1024]{1,0:T(8,128)(2,1)}), bf16[1024,1024]{1,0:T(8,128)(2,1)}) %all-gather.13.cloned.1.call-update) | async-done | bytes 2097168 | tf_op jit(solution)/shard_map/all_gather | solution.py:118
  1078.0 2.9 copy.43
  1086.6 6.5 divide_convert_fusion
  1093.2 290.6 %all-gather.17.cloned.1.call-done = bf16[1024,2048]{1,0:T(8,128)(2,1)} async-done(((bf16[8,2048]{1,0:T(8,128)(2,1)}), bf16[1024,2048]{1,0:T(8,128)(2,1)}) %all-gather.17.cloned.1.call-update) | async-done | bytes 4194320 | tf_op jit(solution)/shard_map/all_gather | solution.py:131
  1383.8 4.4 fusion.11
  (115 shorter events, 77.6 us)
Async XLA Ops:
  6.5 310.6 %copy-start = (bf16[1,256,2048]{2,1,0:T(8,128)(2,1)S(1)}, bf16[1,256,2048]{2,1,0:T(8,128)(2,1)}, u32[]{:S(2)}) copy-start(bf16[1,256,2048]{2,1,0:T(8,128)(2,1)} %param.9) | copy-start | bytes 3145732
  6.5 8.0 copy-start.5
  6.5 310.6 %all-gather.9.cloned.1.call-start = ((), (), s32[]{:S(2)}) async-start(), calls=%async_computation.1 | async-start | bytes 4227072 | tf_op jit(solution)/shard_map/all_gather | solution.py:93
  7.3 617.5 %all-gather.11.cloned.1.call-start = ((), (), s32[]{:S(2)}) async-start(), calls=%async_computation.2 | async-start | bytes 4227072 | tf_op jit(solution)/shard_map/all_gather | solution.py:94
  8.0 925.5 %all-gather.7.cloned.1.call-start = ((), (), s32[]{:S(2)}) async-start(), calls=%async_computation | async-start | bytes 4227072 | tf_op jit(solution)/shard_map/all_gather | solution.py:92
  8.7 997.8 %all-gather.15.cloned.1.call-start = ((), (), s32[]{:S(2)}) async-start(), calls=%async_computation.4 | async-start | bytes 2162688 | tf_op jit(solution)/shard_map/all_gather | solution.py:119
  9.5 615.3 %copy-start.7 = (f32[2048]{0:T(1024)}, f32[2048]{0:T(1024)S(1)}, u32[]{:S(2)}) copy-start(f32[2048]{0:T(1024)S(1)} %convert_element_type.51) | copy-start | bytes 24580
  11.4 613.4 %copy-start.13 = (pred[256]{0:T(512)(128)(4,1)}, pred[256]{0:T(512)(128)(4,1)S(1)}, u32[]{:S(2)}) copy-start(pred[256]{0:T(512)(128)(4,1)S(1)} %broadcast_compare_fusion) | copy-start | bytes 772
  12.9 611.9 %copy-start.9 = (f32[256]{0:T(256)}, f32[256]{0:T(256)S(1)}, u32[]{:S(2)}) copy-start(f32[256]{0:T(256)S(1)} %broadcast_multiply_fusion.2) | copy-start | bytes 3076
  14.6 610.2 %copy-start.11 = (f32[256]{0:T(256)}, f32[256]{0:T(256)S(1)}, u32[]{:S(2)}) copy-start(f32[256]{0:T(256)S(1)} %add_rsqrt_fusion.2) | copy-start | bytes 3076
  320.6 308.5 %copy-start.15 = (bf16[256,1024]{1,0:T(8,128)(2,1)}, bf16[256,1024]{1,0:T(8,128)(2,1)S(1)}, u32[]{:S(2)}) copy-start(bf16[256,1024]{1,0:T(8,128)(2,1)S(1)} %convolution_convert_fusion.1) | copy-start | bytes 1572868
  629.1 5.6 collective-permute-start.1
  698.6 4.3 copy-start.6
  702.8 375.3 %all-gather.13.cloned.1.call-start = ((), (), s32[]{:S(2)}) async-start(), calls=%async_computation.3 | async-start | bytes 2162688 | tf_op jit(solution)/shard_map/all_gather | solution.py:118
  704.4 6.4 collective-permute-start
  775.8 5.5 copy-start.14
  775.8 5.7 copy-start.4
  778.7 154.8 %copy-start.1 = (bf16[1,256,2048]{2,1,0:T(8,128)(2,1)S(1)}, bf16[1,256,2048]{2,1,0:T(8,128)(2,1)}, u32[]{:S(2)}) copy-start(bf16[1,256,2048]{2,1,0:T(8,128)(2,1)} %param.9) | copy-start | bytes 3145732
  778.7 154.7 %copy-start.8 = (f32[2048]{0:T(1024)S(1)}, f32[2048]{0:T(1024)}, u32[]{:S(2)}) copy-start(f32[2048]{0:T(1024)} %copy-done.7) | copy-start | bytes 24580
  778.7 154.7 %copy-start.10 = (f32[256]{0:T(256)S(1)}, f32[256]{0:T(256)}, u32[]{:S(2)}) copy-start(f32[256]{0:T(256)} %copy-done.9) | copy-start | bytes 3076
  778.7 154.7 %copy-start.12 = (f32[256]{0:T(256)S(1)}, f32[256]{0:T(256)}, u32[]{:S(2)}) copy-start(f32[256]{0:T(256)} %copy-done.11) | copy-start | bytes 3076
  780.1 603.7 %all-gather.17.cloned.1.call-start = ((), (), s32[]{:S(2)}) async-start(), calls=%async_computation.5 | async-start | bytes 4227072 | tf_op jit(solution)/shard_map/all_gather | solution.py:131
  781.7 155.3 %copy-start.16 = (bf16[256,1024]{1,0:T(8,128)(2,1)S(1)}, bf16[256,1024]{1,0:T(8,128)(2,1)}, u32[]{:S(2)}) copy-start(bf16[256,1024]{1,0:T(8,128)(2,1)} %copy-done.15) | copy-start | bytes 1572868
  1080.9 1.6 copy-start.3
  1085.1 1.6 copy-start.2
Sparse Core Ops, SparseCore 0:
  9.0 308.0 all-gather.8
  318.8 305.8 all-gather.10
  626.5 306.9 all-gather.6
  936.4 70.0 all-gather.14
  1009.5 68.5 all-gather.12
  1079.6 304.1 all-gather.16
where the time goes:
time: 1400 us
  waiting for transfers between devices  1190 us (85%)
  local copies, waits for them, and re-layouts  139 us (10%)
  matrix products  27 us (2%)
  other arithmetic  17.5 us (1%)
  between operations  14 us (1%)
    all_gather x1, waiting for transfers between devices, on_device(): lax.all_gather(value_weight, ('vid', 'tm'), axis=0, tiled=True)  304 us
    all_gather x1, waiting for transfers between devices, on_device(): lax.all_gather(key_weight, ('vid', 'tm'), axis=0, tiled=True)  302 us
    all_gather x1, waiting for transfers between devices, on_device(): lax.all_gather(out_weight, ('vid', 'tm'), axis=0, tiled=True)  291 us
    all_gather x1, waiting for transfers between devices, on_device(): lax.all_gather(query_weight, ('vid', 'tm'), axis=0, tiled=True)  152 us
    slice x54, local copies, waits for them, and re-layouts, pool_frames(): padded[2 - step_t:2 - step_t + 2 * half_f - 1:2, step_h:step_h + 2 * half...  127 us
    all_gather x1, waiting for transfers between devices, on_device(): lax.all_gather(pooled_value, 'tm', axis=0, tiled=True)  67.7 us
    all_gather x1, waiting for transfers between devices, on_device(): lax.all_gather(pooled_key, 'tm', axis=0, tiled=True)  67.6 us
  transfers between devices with their start and end apart: 8, of which 8 were waited for; matrix products, arithmetic and copies ran while one was open for 13% of the time, Pallas kernels for 0%

commit v1 on v0

v1 whole, which is shorter than its diff:
```python
import functools
import math

import jax
import jax.numpy as jnp
from jax import lax
from jax.experimental import pallas as pl
from jax.experimental.pallas import tpu as pltpu
from jax.sharding import PartitionSpec as P

MESH = pl.DeviceIdType.MESH
HEADS = 8
HD = 128
SIDE = 8
SPATIAL = SIDE * SIDE
N_TM = 32
ROWS = 256
FRAMES_DEV = ROWS // SPATIAL
EXT = ROWS + SPATIAL
MEM_DEV = 32
D = 2048
WIDTH = HEADS * HD
NEG = -1e30
SCALE = (1.0 / math.sqrt(HD)) * math.log2(math.e)

STREAMS = (
    (
        (1, 0, 768, "xyz"),
        (1, 768, 256, "yzx"),
        (2, 0, 384, "yzx"),
        (2, 384, 640, "zxy"),
    ),
    (
        (0, 0, 640, "xyz"),
        (0, 640, 384, "yzx"),
        (3, 0, 512, "yzx"),
        (3, 512, 1536, "zxy"),
    ),
)
PIECES = STREAMS[0] + STREAMS[1]
MEMORY_ORDERS = ("xy", "yx")


def device(place, core):
    x, y, z = place["x"], place["y"], place["z"]
    return (lax.rem(z, 2) * 2 + core, x * 8 + (z // 2) * 4 + y)


def moved(place, axis, steps):
    return {**place, axis: lax.rem(place[axis] + steps + 4, 4)}


def halves(start, size):
    first = (size // 256) * 128 if size > 128 else size
    first = size - first
    return ((start, first), (start + first, size - first))


class Wires:
    def __init__(self, send_sems, recv_sems):
        self.send_sems, self.recv_sems = send_sems, recv_sems
        self.count = 0
        self.started = []

    def slot(self):
        self.count += 1
        return self.count - 1

    def send(self, slot, src, dst, target):
        copy = pltpu.make_async_remote_copy(
            src_ref=src,
            dst_ref=dst,
            send_sem=self.send_sems.at[slot],
            recv_sem=self.recv_sems.at[slot],
            device_id=target,
            device_id_type=MESH,
        )
        copy.start()
        self.started.append(copy)

    def receive(self, slot, dst, source):
        pltpu.make_async_remote_copy(
            src_ref=dst,
            dst_ref=dst,
            send_sem=self.send_sems.at[slot],
            recv_sem=self.recv_sems.at[slot],
            device_id=source,
            device_id_type=MESH,
        ).wait_recv()

    def drain(self):
        for copy in self.started:
            copy.wait_send()


def weight_view(ref, core, place, start, size):
    every = slice(None)
    x, y, z = (place[axis] for axis in "xyz")
    zl = every if z is None else lax.rem(z, 2)
    zh = every if z is None else z // 2
    return ref.at[
        zl,
        core,
        every if x is None else x,
        zh,
        every if y is None else y,
        :,
        pl.ds(start, size),
    ]


def memory_view(ref, place, start, size):
    every = slice(None)
    x, y, z = (place[axis] for axis in "xyz")
    return ref.at[
        every if x is None else x,
        every if z is None else z // 2,
        every if y is None else y,
        :,
        pl.ds(start, size),
    ]


class Ring:
    def __init__(self, wires, view, place, core, axis, known, start, size):
        self.wires, self.place, self.core, self.axis = wires, place, core, axis
        self.known, self.start, self.size = known, start, size
        self.view = view
        self.slots = [wires.slot() for _ in range(4)]

    def region(self, steps, start, size):
        place = {**moved(self.place, self.axis, steps), **{a: None for a in self.known}}
        return self.view(place, start, size)

    def target(self, steps):
        return device(moved(self.place, self.axis, steps), self.core)

    def open(self, src=None):
        mine = self.region(0, self.start, self.size)
        for slot, steps in zip(self.slots[:2], (1, -1)):
            self.wires.send(slot, mine if src is None else src, mine, self.target(steps))

    def relay(self):
        for slot, steps, part in zip(self.slots[:2], (1, -1), halves(self.start, self.size)):
            self.wires.receive(slot, self.region(-steps, self.start, self.size), self.target(-steps))
        for slot, steps, part in zip(self.slots[2:], (1, -1), halves(self.start, self.size)):
            region = self.region(-steps, *part)
            self.wires.send(slot, region, region, self.target(steps))

    def close(self):
        for slot, steps, part in zip(self.slots[2:], (1, -1), halves(self.start, self.size)):
            self.wires.receive(slot, self.region(2, *part), self.target(-steps))


class Gather:
    def __init__(self, wires, ref, shard, place, core, piece):
        _, self.start, self.size, order = piece
        self.wires, self.ref, self.shard = wires, ref, shard
        self.place, self.core, self.order = place, core, order
        self.partner = device(place, 1 - core)
        self.rings = [
            Ring(
                wires,
                lambda at, start, size: weight_view(ref, core, at, start, size),
                place,
                core,
                axis,
                order[:k],
                self.start,
                self.size,
            )
            for k, axis in enumerate(order)
        ]
        self.slots = [wires.slot() for _ in range(4)]

    def open(self):
        self.rings[0].open(self.shard.at[:, pl.ds(self.start, self.size)])

    def relay(self, k):
        self.rings[k].relay()

    def close(self, k):
        self.rings[k].close()
        if k < 2:
            self.rings[k + 1].open()

    def region(self, core, steps):
        place = {
            **moved(self.place, self.order[2], steps),
            self.order[0]: None,
            self.order[1]: None,
        }
        return weight_view(self.ref, core, place, self.start, self.size)

    def hand(self, k):
        region = self.region(self.core, (0, 1, -1, 2)[k])
        self.wires.send(self.slots[k], region, region, self.partner)

    def take(self):
        for k, steps in enumerate((0, 1, -1, 2)):
            self.wires.receive(self.slots[k], self.region(1 - self.core, steps), self.partner)


def normalize_rows(values, gain):
    center = jnp.mean(values, axis=-1, keepdims=True)
    spread = jnp.mean((values - center) ** 2, axis=-1, keepdims=True)
    return ((values - center) * lax.rsqrt(spread + 1e-06) * gain).astype(jnp.bfloat16)


def project(normed, first, count, weight, out):
    def tile(j, carry):
        columns = pl.ds(pl.multiple_of(j * 256, 256), 256)
        total = jnp.zeros((count, 256), jnp.float32)
        for vid in range(4):
            rows = weight[vid // 2, vid % 2, :, :, :, :, columns].reshape(512, 256)
            total = total + jnp.dot(
                normed[first : first + count, vid * 512 : (vid + 1) * 512],
                rows,
                preferred_element_type=jnp.float32,
            )
        out[:, columns] = total.astype(jnp.bfloat16)
        return carry

    lax.fori_loop(0, WIDTH // 256, tile, 0)


def pool(source, taps, valid, spread_tmp, out, place):
    column = lax.broadcasted_iota(jnp.int32, (SIDE, HD), 0)

    def head(h, carry):
        lanes = pl.ds(pl.multiple_of(h * HD, HD), HD)
        grid = source[:, lanes].astype(jnp.float32).reshape(FRAMES_DEV + 1, SIDE, SIDE, HD)
        kernel = taps[:, lanes].astype(jnp.float32)
        frames = [jnp.where(valid[f], grid[f], 0.0) for f in range(FRAMES_DEV + 1)]
        for j in range(FRAMES_DEV // 2):
            for a in range(SIDE // 2):
                sums = [jnp.zeros((SIDE, HD), jnp.float32) for _ in range(3)]
                for dt in range(3):
                    for dh in range(3):
                        row = 2 * a + dh - 1
                        if row < 0:
                            continue
                        values = frames[2 * j + 2 - dt][row]
                        for dw in range(3):
                            tap = 9 * dt + 3 * dh + dw
                            sums[dw] = sums[dw] + values * kernel[tap : tap + 1]
                left = jnp.where(column == 0, 0.0, pltpu.roll(sums[0], 1, 0))
                right = pltpu.roll(sums[2], SIDE - 1, 0)
                at = (j * (SIDE // 2) + a) * SIDE
                spread_tmp[h, at : at + SIDE, :] = sums[1] + left + right
        rows = spread_tmp[h, pl.ds(0, MEM_DEV, stride=2), :]
        center = jnp.mean(rows, axis=-1, keepdims=True)
        width = jnp.mean((rows - center) ** 2, axis=-1, keepdims=True)
        normed = (rows - center) * lax.rsqrt(width + 1e-06)
        out[place["x"], place["z"] // 2, place["y"], :, lanes] = normed.astype(jnp.bfloat16)
        return carry

    lax.fori_loop(0, HEADS, head, 0)


def scores_of(queries, keys):
    return lax.dot_general(
        queries, keys, (((1,), (1,)), ((), ())), preferred_element_type=jnp.float32
    )


def weighted(weights, values):
    high = weights.astype(jnp.bfloat16)
    low = (weights - high.astype(jnp.float32)).astype(jnp.bfloat16)
    return jnp.dot(high, values, preferred_element_type=jnp.float32) + jnp.dot(
        low, values, preferred_element_type=jnp.float32
    )


def body(
    video,
    gain,
    query_shard,
    key_shard,
    value_shard,
    key_taps,
    value_taps,
    out_shard,
    frames_valid,
    out,
    tokens,
    normed,
    query_w,
    key_w,
    value_w,
    out_w,
    out_rows,
    query,
    key,
    value,
    memory_key,
    memory_value,
    spread_key,
    spread_value,
    heads,
    local_sems,
    send_sems,
    recv_sems,
):
    vid, tm = lax.axis_index("vid"), lax.axis_index("tm")
    core = lax.rem(vid, 2)
    place = {
        "x": tm // 8,
        "y": lax.rem(tm, 4),
        "z": lax.rem(tm // 4, 2) * 2 + vid // 2,
    }
    after, before = lax.rem(tm + 1, N_TM), lax.rem(tm + N_TM - 1, N_TM)
    partner = device(place, 1 - core)
    across = device(moved(place, "z", 2), core)

    barrier = pltpu.get_barrier_semaphore()
    greeted = [device(moved(place, axis, steps), core) for axis in "xyz" for steps in (1, -1)]
    greeted += [partner, across, (vid, after), (vid, before)]
    for other in greeted:
        pl.semaphore_signal(barrier, inc=1, device_id=other, device_id_type=MESH)

    shards = (query_shard, key_shard, value_shard, out_shard)
    weights = (query_w, key_w, value_w, out_w)
    own = [
        pltpu.make_async_copy(
            shard,
            weight.at[vid // 2, core, place["x"], place["z"] // 2, place["y"]],
            local_sems.at[k],
        )
        for k, (shard, weight) in enumerate(zip(shards, weights))
    ]
    own_tokens = pltpu.make_async_copy(video, tokens.at[pl.ds(SPATIAL, ROWS)], local_sems.at[4])
    for copy in own:
        copy.start()
    own_tokens.start()
    pl.semaphore_wait(barrier, len(greeted))

    wires = Wires(send_sems, recv_sems)
    streams = [
        [Gather(wires, weights[p[0]], shards[p[0]], place, core, p) for p in stream]
        for stream in STREAMS
    ]
    for stream in streams:
        for gather in stream:
            gather.open()
    halo_slot = wires.slot()
    halo = tokens.at[pl.ds(0, SPATIAL)]
    wires.send(halo_slot, video.at[pl.ds(ROWS - SPATIAL, SPATIAL)], halo, (vid, after))
    for copy in own:
        copy.wait()
    own_tokens.wait()

    scale = gain[...].astype(jnp.float32)

    def normalize_at(i, carry):
        at = pl.ds(pl.multiple_of(i * 32, 32), 32)
        normed[at, :] = normalize_rows(tokens[at, :].astype(jnp.float32), scale)
        return carry

    for k in range(3):
        for stream in streams:
            for gather in stream:
                gather.relay(k)
        if k == 0:
            lax.fori_loop(SPATIAL // 32, EXT // 32, normalize_at, 0)
        if k == 1:
            wires.receive(halo_slot, halo, (vid, before))
            lax.fori_loop(0, SPATIAL // 32, normalize_at, 0)
        if k == 2:
            for stream in streams:
                for gather in stream:
                    gather.hand(0)
                    gather.hand(1)
                    gather.hand(2)
        for number, stream in enumerate(streams):
            for gather in stream:
                gather.close(k)
            if k == 2:
                for gather in stream:
                    gather.hand(3)
                for gather in stream:
                    gather.take()
                if number == 0:
                    project(normed, 0, EXT, key_w, key)
                    project(normed, 0, EXT, value_w, value)
                else:
                    project(normed, SPATIAL, ROWS, query_w, query)

    limit = frames_valid[vid]
    first_frame = tm * FRAMES_DEV
    valid = [
        (first_frame + f - 1 < limit) & (first_frame + f - 1 >= 0) for f in range(FRAMES_DEV + 1)
    ]
    pool(key, key_taps, valid, spread_key, memory_key, place)
    pool(value, value_taps, valid, spread_value, memory_value, place)

    memory = []
    for ref, order in zip((memory_key, memory_value), MEMORY_ORDERS):
        region = memory_view(ref, place, 0, WIDTH)
        slot = wires.slot()
        wires.send(slot, region, region, across)
        rings = [
            Ring(
                wires,
                functools.partial(
                    lambda at_ref, at, start, size: memory_view(at_ref, at, start, size), ref
                ),
                place,
                core,
                axis,
                "z" + order[:k],
                0,
                WIDTH,
            )
            for k, axis in enumerate(order)
        ]
        memory.append((ref, slot, rings))

    def out_tile(j, carry):
        columns = pl.ds(pl.multiple_of(j * 256, 256), 256)
        out_rows[:, columns] = (
            out_w[:, :, :, :, :, :, columns]
            .astype(jnp.float32)
            .reshape(WIDTH, 256)
            .astype(jnp.bfloat16)
        )
        return carry

    lax.fori_loop(0, D // 256, out_tile, 0)

    for ref, slot, rings in memory:
        wires.receive(slot, memory_view(ref, moved(place, "z", 2), 0, WIDTH), across)
        rings[0].open()
    for k in range(2):
        for _, _, rings in memory:
            rings[k].relay()
        for _, _, rings in memory:
            rings[k].close()
            if k == 0:
                rings[1].open()

    query_frame = lax.broadcasted_iota(jnp.int32, (ROWS, ROWS), 0) // SPATIAL
    key_frame = lax.broadcasted_iota(jnp.int32, (ROWS, ROWS), 1) // SPATIAL
    near = (key_frame <= query_frame) & (first_frame + key_frame < limit)
    near_bias = jnp.where(near, 0.0, NEG)
    index = lax.broadcasted_iota(jnp.int32, (1, N_TM * MEM_DEV), 1)
    far = (2 * (index // (SPATIAL // 4)) < limit) & (index // MEM_DEV <= tm)
    far_bias = jnp.where(far, 0.0, NEG)

    def attend(h, carry):
        lanes = pl.ds(pl.multiple_of(h * HD, HD), HD)
        queries = query[:, lanes]
        far_keys = memory_key[:, :, :, :, lanes].reshape(N_TM * MEM_DEV, HD)
        far_values = memory_value[:, :, :, :, lanes].reshape(N_TM * MEM_DEV, HD)
        near_scores = scores_of(queries, key[SPATIAL:, lanes]) * SCALE + near_bias
        far_scores = scores_of(queries, far_keys) * SCALE + far_bias
        top = jnp.maximum(
            jnp.max(near_scores, axis=-1, keepdims=True),
            jnp.max(far_scores, axis=-1, keepdims=True),
        )
        near_weights = jnp.exp2(near_scores - top)
        far_weights = jnp.exp2(far_scores - top)
        total = jnp.sum(near_weights, axis=-1, keepdims=True) + jnp.sum(
            far_weights, axis=-1, keepdims=True
        )
        mixed = weighted(near_weights, value[SPATIAL:, lanes]) + weighted(far_weights, far_values)
        heads[:, lanes] = (mixed / total).astype(jnp.bfloat16)
        return carry

    lax.fori_loop(0, HEADS, attend, 0)

    row_frame = first_frame + lax.broadcasted_iota(jnp.int32, (ROWS, 1), 0) // SPATIAL

    def result_tile(j, carry):
        columns = pl.ds(pl.multiple_of(j * 256, 256), 256)
        result = jnp.dot(heads[...], out_rows[:, columns], preferred_element_type=jnp.float32)
        out[:, columns] = jnp.where(row_frame < limit, result, 0.0).astype(jnp.bfloat16)
        return carry

    lax.fori_loop(0, D // 256, result_tile, 0)
    wires.drain()


N_SLOTS = len(PIECES) * 16 + 1 + 2 * 9


def on_device(
    video,
    norm_gain,
    query_weight,
    key_weight,
    value_weight,
    key_kernel,
    value_kernel,
    out_weight,
    frames_valid,
):
    bf16 = jnp.bfloat16
    gathered = (2, 2, 4, 2, 4)
    vmem = pl.BlockSpec(memory_space=pltpu.VMEM)
    hbm = pl.BlockSpec(memory_space=pl.ANY)
    result = pl.pallas_call(
        body,
        out_shape=jax.ShapeDtypeStruct((ROWS, D), bf16),
        in_specs=[
            hbm,
            vmem,
            hbm,
            hbm,
            hbm,
            vmem,
            vmem,
            hbm,
            pl.BlockSpec(memory_space=pltpu.SMEM),
        ],
        out_specs=vmem,
        scratch_shapes=[
            pltpu.VMEM((EXT, D), bf16),
            pltpu.VMEM((EXT, D), bf16),
            pltpu.VMEM((*gathered, 16, WIDTH), bf16),
            pltpu.VMEM((*gathered, 16, WIDTH), bf16),
            pltpu.VMEM((*gathered, 16, WIDTH), bf16),
            pltpu.VMEM((*gathered, 8, D), bf16),
            pltpu.VMEM((WIDTH, D), bf16),
            pltpu.VMEM((ROWS, WIDTH), bf16),
            pltpu.VMEM((EXT, WIDTH), bf16),
            pltpu.VMEM((EXT, WIDTH), bf16),
            pltpu.VMEM((4, 2, 4, MEM_DEV, WIDTH), bf16),
            pltpu.VMEM((4, 2, 4, MEM_DEV, WIDTH), bf16),
            pltpu.VMEM((HEADS, 2 * MEM_DEV, HD), jnp.float32),
            pltpu.VMEM((HEADS, 2 * MEM_DEV, HD), jnp.float32),
            pltpu.VMEM((ROWS, WIDTH), bf16),
            pltpu.SemaphoreType.DMA((5,)),
            pltpu.SemaphoreType.DMA((N_SLOTS,)),
            pltpu.SemaphoreType.DMA((N_SLOTS,)),
        ],
        compiler_params=pltpu.CompilerParams(
            collective_id=0, has_side_effects=True, vmem_limit_bytes=60 * 1024 * 1024
        ),
        name="memory_attention",
    )(
        video[0],
        norm_gain.reshape(1, D),
        query_weight,
        key_weight,
        value_weight,
        key_kernel,
        value_kernel,
        out_weight,
        frames_valid,
    )
    return result[None]


def solution(mesh):
    in_specs = (
        P("vid", "tm", None),
        P(),
        P(("vid", "tm"), None),
        P(("vid", "tm"), None),
        P(("vid", "tm"), None),
        P(),
        P(),
        P(("vid", "tm"), None),
        P(),
    )
    out_specs = P("vid", "tm", None)
    return jax.shard_map(
        on_device, mesh=mesh, in_specs=in_specs, out_specs=out_specs, check_vma=False
    )
```

time: 1400 us -> 121 us (0.09)
  the two profiles are of different devices: /device:TPU:1 before, /device:TPU:0 now
where the time goes in v1:
time: 121 us; the launch traced here: 120 us
  Pallas kernels  117 us (97%)
  local copies, waits for them, and re-layouts  3.59 us (3%)
    pallas_call x1, Pallas kernels, on_device(): pl.pallas_call(body, out_shape=jax.ShapeDtypeStruct((ROWS, D), bf16), in_...  117 us

profile of v1, /device:TPU:0, one launch (start us, length us, event | category | flops | bytes accessed | tf_op | source)
XLA Modules:
  0.0 120.4 jit_solution(15489374089217017801)
XLA Ops:
  0.0 1.3 %reshape.3.gain = bf16[1,2048]{1,0:T(2,128)(2,1)} reshape(bf16[2048]{0:T(1024)(128)(2,1)} %param.10) | data formatting | bytes 8192 | tf_op jit(solution)/shard_map/reshape | solution.py:543
  1.3 116.8 %memory_attention.1 = bf16[256,2048]{1,0:T(8,128)(2,1)} custom-call(bf16[256,2048]{1,0:T(8,128)(2,1)} %bitcast.3, bf16[1,2048]{1,0:T(2,128)(2,1)} %reshape.3.gain, bf16[16,1024]{1,0:T(8,128)(2,1)} %query_shard.1, bf16[16,1024]{1,0:T(8,128)(2,1)} %key_shard.1, bf16[16,1024]{1,0:T(8,128)(2,1)} %value_shard.1, bf16[27,1024]{1,0:T(8,128)(2,1)} %key_taps.1, ...), custom_call_target="tpu_custom_call" | custom-call | tf_op jit(solution)/shard_map/memory_attention/pallas_call | solution.py:502
  118.1 2.3 %copy.11 = bf16[1,256,2048]{2,1,0:T(8,128)(2,1)} copy(bf16[1,256,2048]{2,1,0:T(8,128)(2,1)} %bitcast.2) | data formatting | bytes 2097152

commit v2 on v1

--- a/solution.py
+++ b/solution.py
@@ -23,22 +23,18 @@
 NEG = -1e30
 SCALE = (1.0 / math.sqrt(HD)) * math.log2(math.e)
 
-STREAMS = (
-    (
-        (1, 0, 768, "xyz"),
-        (1, 768, 256, "yzx"),
-        (2, 0, 384, "yzx"),
-        (2, 384, 640, "zxy"),
-    ),
-    (
-        (0, 0, 640, "xyz"),
-        (0, 640, 384, "yzx"),
-        (3, 0, 512, "yzx"),
-        (3, 512, 1536, "zxy"),
-    ),
+KEY_VALUE = (
+    (1, 0, 768, "xyz"),
+    (1, 768, 256, "yzx"),
+    (2, 0, 384, "yzx"),
+    (2, 384, 640, "zxy"),
 )
-PIECES = STREAMS[0] + STREAMS[1]
+QUERY = ((0, 0, 384, "xyz"), (0, 384, 384, "yzx"), (0, 768, 256, "zxy"))
+OUT = ((3, 0, 1024, "xyz"), (3, 1024, 1024, "yxz"))
+PIECES = KEY_VALUE + QUERY + OUT
+HALF = WIDTH // 2
 MEMORY_ORDERS = ("xy", "yx")
+KEYS = ROWS + N_TM * MEM_DEV
 
 
 def device(place, core):
@@ -66,7 +62,7 @@
         self.count += 1
         return self.count - 1
 
-    def send(self, slot, src, dst, target):
+    def send(self, slot, src, dst, target, start=True):
         copy = pltpu.make_async_remote_copy(
             src_ref=src,
             dst_ref=dst,
@@ -75,8 +71,10 @@
             device_id=target,
             device_id_type=MESH,
         )
-        copy.start()
+        if start:
+            copy.start()
         self.started.append(copy)
+        return copy
 
     def receive(self, slot, dst, source):
         pltpu.make_async_remote_copy(
@@ -122,14 +120,15 @@
 
 
 class Ring:
-    def __init__(self, wires, view, place, core, axis, known, start, size):
+    def __init__(self, wires, view, place, core, axis, known, start, size, source=None):
         self.wires, self.place, self.core, self.axis = wires, place, core, axis
+        self.source = place if source is None else source
         self.known, self.start, self.size = known, start, size
         self.view = view
         self.slots = [wires.slot() for _ in range(4)]
 
     def region(self, steps, start, size):
-        place = {**moved(self.place, self.axis, steps), **{a: None for a in self.known}}
+        place = {**moved(self.source, self.axis, steps), **{a: None for a in self.known}}
         return self.view(place, start, size)
 
     def target(self, steps):
@@ -181,8 +180,11 @@
 
     def close(self, k):
         self.rings[k].close()
-        if k < 2:
-            self.rings[k + 1].open()
+        if k == 0:
+            self.rings[1].open()
+
+    def last(self):
+        self.rings[2].open()
 
     def region(self, core, steps):
         place = {
@@ -207,18 +209,20 @@
     return ((values - center) * lax.rsqrt(spread + 1e-06) * gain).astype(jnp.bfloat16)
 
 
-def project(normed, first, count, weight, out):
+def project(normed, first, count, weight, core, partial, out):
     def tile(j, carry):
         columns = pl.ds(pl.multiple_of(j * 256, 256), 256)
-        total = jnp.zeros((count, 256), jnp.float32)
-        for vid in range(4):
-            rows = weight[vid // 2, vid % 2, :, :, :, :, columns].reshape(512, 256)
+        total = jnp.zeros((count, 256), jnp.float32) if out is None else partial[:count, columns]
+        for zl in range(2):
+            rows = weight[zl, core, :, :, :, :, columns].reshape(512, 256)
+            depth = pl.ds(pl.multiple_of((zl * 2 + core) * 512, 512), 512)
             total = total + jnp.dot(
-                normed[first : first + count, vid * 512 : (vid + 1) * 512],
-                rows,
-                preferred_element_type=jnp.float32,
+                normed[first : first + count, depth], rows, preferred_element_type=jnp.float32
             )
-        out[:, columns] = total.astype(jnp.bfloat16)
+        if out is None:
+            partial[:count, columns] = total
+        else:
+            out[:, columns] = total.astype(jnp.bfloat16)
         return carry
 
     lax.fori_loop(0, WIDTH // 256, tile, 0)
@@ -264,12 +268,33 @@
     )
 
 
-def weighted(weights, values):
-    high = weights.astype(jnp.bfloat16)
-    low = (weights - high.astype(jnp.float32)).astype(jnp.bfloat16)
-    return jnp.dot(high, values, preferred_element_type=jnp.float32) + jnp.dot(
-        low, values, preferred_element_type=jnp.float32
-    )
+class Memory:
+    def __init__(self, wires, ref, place, core, order, start, own):
+        self.rings = [
+            Ring(
+                wires,
+                lambda at, first, size: memory_view(ref, at, first, size),
+                place,
+                core,
+                axis,
+                order[:k],
+                start,
+                HALF,
+                place if own else moved(place, "z", 2),
+            )
+            for k, axis in enumerate(order)
+        ]
+
+    def open(self):
+        self.rings[0].open()
+
+    def relay(self, k):
+        self.rings[k].relay()
+
+    def close(self, k):
+        self.rings[k].close()
+        if k == 0:
+            self.rings[1].open()
 
 
 def body(
@@ -290,6 +315,8 @@
     value_w,
     out_w,
     out_rows,
+    key_partial,
+    value_partial,
     query,
     key,
     value,
@@ -297,6 +324,9 @@
     memory_value,
     spread_key,
     spread_value,
+    highs,
+    lows,
+    totals,
     heads,
     local_sems,
     send_sems,
@@ -315,7 +345,7 @@
 
     barrier = pltpu.get_barrier_semaphore()
     greeted = [device(moved(place, axis, steps), core) for axis in "xyz" for steps in (1, -1)]
-    greeted += [partner, across, (vid, after), (vid, before)]
+    greeted.append(partner)
     for other in greeted:
         pl.semaphore_signal(barrier, inc=1, device_id=other, device_id_type=MESH)
 
@@ -336,85 +366,189 @@
     pl.semaphore_wait(barrier, len(greeted))
 
     wires = Wires(send_sems, recv_sems)
-    streams = [
+    key_value, query_part, out_part = (
         [Gather(wires, weights[p[0]], shards[p[0]], place, core, p) for p in stream]
-        for stream in STREAMS
-    ]
-    for stream in streams:
-        for gather in stream:
-            gather.open()
+        for stream in (KEY_VALUE, QUERY, OUT)
+    )
+    everything = key_value + query_part + out_part
+    for gather in everything:
+        gather.open()
     halo_slot = wires.slot()
     halo = tokens.at[pl.ds(0, SPATIAL)]
-    wires.send(halo_slot, video.at[pl.ds(ROWS - SPATIAL, SPATIAL)], halo, (vid, after))
+
+    last_frame = video.at[pl.ds(ROWS - SPATIAL, SPATIAL)]
+    halo_copy = wires.send(halo_slot, last_frame, halo, (vid, after), start=False)
+
+    @pl.when(place["y"] < 3)
+    def _():
+        halo_copy.start()
+
     for copy in own:
         copy.wait()
     own_tokens.wait()
 
-    scale = gain[...].astype(jnp.float32)
+    scale = gain[...].astype(jnp.float32).reshape(1, D)
 
     def normalize_at(i, carry):
         at = pl.ds(pl.multiple_of(i * 32, 32), 32)
         normed[at, :] = normalize_rows(tokens[at, :].astype(jnp.float32), scale)
         return carry
 
-    for k in range(3):
-        for stream in streams:
-            for gather in stream:
-                gather.relay(k)
-        if k == 0:
-            lax.fori_loop(SPATIAL // 32, EXT // 32, normalize_at, 0)
-        if k == 1:
-            wires.receive(halo_slot, halo, (vid, before))
-            lax.fori_loop(0, SPATIAL // 32, normalize_at, 0)
-        if k == 2:
-            for stream in streams:
-                for gather in stream:
-                    gather.hand(0)
-                    gather.hand(1)
-                    gather.hand(2)
-        for number, stream in enumerate(streams):
-            for gather in stream:
-                gather.close(k)
-            if k == 2:
-                for gather in stream:
-                    gather.hand(3)
-                for gather in stream:
-                    gather.take()
-                if number == 0:
-                    project(normed, 0, EXT, key_w, key)
-                    project(normed, 0, EXT, value_w, value)
-                else:
-                    project(normed, SPATIAL, ROWS, query_w, query)
+    lax.fori_loop(SPATIAL // 32, EXT // 32, normalize_at, 0)
+    for k in range(2):
+        for gather in everything:
+            gather.relay(k)
+        for gather in everything:
+            gather.close(k)
+            if k == 1 and gather in key_value:
+                gather.last()
+
+    @pl.when(place["y"] == 3)
+    def _():
+        halo_copy.start()
+
+    for gather in key_value:
+        gather.hand(0)
+    for gather in key_value:
+        gather.relay(2)
+        gather.hand(1)
+        gather.hand(2)
+    for gather in query_part:
+        gather.last()
+        gather.hand(0)
+    wires.receive(halo_slot, halo, (vid, before))
+    lax.fori_loop(0, SPATIAL // 32, normalize_at, 0)
+    for gather in key_value:
+        gather.close(2)
+        gather.hand(3)
+    project(normed, 0, EXT, key_w, core, key_partial, None)
+    project(normed, 0, EXT, value_w, core, value_partial, None)
+    for gather in key_value:
+        gather.take()
+    for gather in query_part:
+        gather.relay(2)
+        gather.hand(1)
+        gather.hand(2)
+    project(normed, 0, EXT, key_w, 1 - core, key_partial, key)
+    project(normed, 0, EXT, value_w, 1 - core, value_partial, value)
 
     limit = frames_valid[vid]
     first_frame = tm * FRAMES_DEV
     valid = [
         (first_frame + f - 1 < limit) & (first_frame + f - 1 >= 0) for f in range(FRAMES_DEV + 1)
     ]
-    pool(key, key_taps, valid, spread_key, memory_key, place)
-    pool(value, value_taps, valid, spread_value, memory_value, place)
-
-    memory = []
-    for ref, order in zip((memory_key, memory_value), MEMORY_ORDERS):
+    memories = []
+    for source, taps, spread, ref in (
+        (key, key_taps, spread_key, memory_key),
+        (value, value_taps, spread_value, memory_value),
+    ):
+        pool(source, taps, valid, spread, ref, place)
         region = memory_view(ref, place, 0, WIDTH)
         slot = wires.slot()
+        parts = [
+            [
+                Memory(wires, ref, place, core, order, number * HALF, own_plane)
+                for number, order in enumerate(MEMORY_ORDERS)
+            ]
+            for own_plane in (True, False)
+        ]
+        for part in parts[0]:
+            part.open()
         wires.send(slot, region, region, across)
-        rings = [
-            Ring(
-                wires,
-                functools.partial(
-                    lambda at_ref, at, start, size: memory_view(at_ref, at, start, size), ref
-                ),
-                place,
-                core,
-                axis,
-                "z" + order[:k],
-                0,
-                WIDTH,
+        memories.append((ref, slot, parts))
+        if ref is memory_key:
+            for gather in query_part:
+                gather.close(2)
+                gather.hand(3)
+    for gather in out_part:
+        gather.last()
+        gather.hand(0)
+
+    for ref, slot, (mine, other) in memories:
+        for part in mine:
+            part.relay(0)
+        wires.receive(slot, memory_view(ref, moved(place, "z", 2), 0, WIDTH), across)
+        for part in other:
+            part.open()
+        for part in mine:
+            part.close(0)
+    for gather in query_part:
+        gather.take()
+    project(normed, SPATIAL, ROWS, query_w, core, key_partial, None)
+    for _, _, (mine, other) in memories:
+        for part in other:
+            part.relay(0)
+        for part in other:
+            part.close(0)
+    for _, _, (mine, other) in memories:
+        for part in mine:
+            part.relay(1)
+    for gather in out_part:
+        gather.relay(2)
+        gather.hand(1)
+        gather.hand(2)
+    project(normed, SPATIAL, ROWS, query_w, 1 - core, key_partial, query)
+    for _, _, (mine, other) in memories:
+        for part in other:
+            part.relay(1)
+    for part in memories[0][2][0] + memories[0][2][1]:
+        part.close(1)
+
+    query_frame = lax.broadcasted_iota(jnp.int32, (ROWS, ROWS), 0) // SPATIAL
+    key_frame = lax.broadcasted_iota(jnp.int32, (ROWS, ROWS), 1) // SPATIAL
+    near = (key_frame <= query_frame) & (first_frame + key_frame < limit)
+    near_bias = jnp.where(near, 0.0, NEG)
+    index = lax.broadcasted_iota(jnp.int32, (1, N_TM * MEM_DEV), 1)
+    far = (2 * (index // (SPATIAL // 4)) < limit) & (index // MEM_DEV <= tm)
+    far_bias = jnp.where(far, 0.0, NEG)
+
+    def weigh(h, carry):
+        lanes = pl.ds(pl.multiple_of(h * HD, HD), HD)
+        queries = query[:, lanes]
+        far_keys = memory_key[:, :, :, :, lanes].reshape(N_TM * MEM_DEV, HD)
+        near_scores = scores_of(queries, key[SPATIAL:, lanes]) * SCALE + near_bias
+        far_scores = scores_of(queries, far_keys) * SCALE + far_bias
+        top = jnp.maximum(
+            jnp.max(near_scores, axis=-1, keepdims=True),
+            jnp.max(far_scores, axis=-1, keepdims=True),
+        )
+        total = jnp.zeros((ROWS, 1), jnp.float32)
+        for first, scores in ((0, near_scores), (ROWS, far_scores)):
+            exps = jnp.exp2(scores - top)
+            total = total + jnp.sum(exps, axis=-1, keepdims=True)
+            high = exps.astype(jnp.bfloat16)
+            low = (exps - high.astype(jnp.float32)).astype(jnp.bfloat16)
+            highs[h, :, first : first + scores.shape[1]] = high
+            lows[h, :, first : first + scores.shape[1]] = low
+        totals[h] = jnp.broadcast_to(total, (ROWS, HD))
+        return carry
+
+    lax.fori_loop(0, HEADS, weigh, 0)
+
+    for part in memories[1][2][0] + memories[1][2][1]:
+        part.close(1)
+    for gather in out_part:
+        gather.close(2)
+        gather.hand(3)
+
+    def mix(h, carry):
+        lanes = pl.ds(pl.multiple_of(h * HD, HD), HD)
+        near_values = value[SPATIAL:, lanes]
+        far_values = memory_value[:, :, :, :, lanes].reshape(N_TM * MEM_DEV, HD)
+        mixed = jnp.zeros((ROWS, HD), jnp.float32)
+        for part in (highs, lows):
+            mixed = mixed + jnp.dot(
+                part[h, :, :ROWS], near_values, preferred_element_type=jnp.float32
             )
-            for k, axis in enumerate(order)
-        ]
-        memory.append((ref, slot, rings))
+            mixed = mixed + jnp.dot(
+                part[h, :, ROWS:], far_values, preferred_element_type=jnp.float32
+            )
+        heads[:, lanes] = (mixed / totals[h]).astype(jnp.bfloat16)
+        return carry
+
+    lax.fori_loop(0, HEADS, mix, 0)
+    for gather in out_part:
+        gather.take()
 
     def out_tile(j, carry):
         columns = pl.ds(pl.multiple_of(j * 256, 256), 256)
@@ -428,47 +562,6 @@
 
     lax.fori_loop(0, D // 256, out_tile, 0)
 
-    for ref, slot, rings in memory:
-        wires.receive(slot, memory_view(ref, moved(place, "z", 2), 0, WIDTH), across)
-        rings[0].open()
-    for k in range(2):
-        for _, _, rings in memory:
-            rings[k].relay()
-        for _, _, rings in memory:
-            rings[k].close()
-            if k == 0:
-                rings[1].open()
-
-    query_frame = lax.broadcasted_iota(jnp.int32, (ROWS, ROWS), 0) // SPATIAL
-    key_frame = lax.broadcasted_iota(jnp.int32, (ROWS, ROWS), 1) // SPATIAL
-    near = (key_frame <= query_frame) & (first_frame + key_frame < limit)
-    near_bias = jnp.where(near, 0.0, NEG)
-    index = lax.broadcasted_iota(jnp.int32, (1, N_TM * MEM_DEV), 1)
-    far = (2 * (index // (SPATIAL // 4)) < limit) & (index // MEM_DEV <= tm)
-    far_bias = jnp.where(far, 0.0, NEG)
-
-    def attend(h, carry):
-        lanes = pl.ds(pl.multiple_of(h * HD, HD), HD)
-        queries = query[:, lanes]
-        far_keys = memory_key[:, :, :, :, lanes].reshape(N_TM * MEM_DEV, HD)
-        far_values = memory_value[:, :, :, :, lanes].reshape(N_TM * MEM_DEV, HD)
-        near_scores = scores_of(queries, key[SPATIAL:, lanes]) * SCALE + near_bias
-        far_scores = scores_of(queries, far_keys) * SCALE + far_bias
-        top = jnp.maximum(
-            jnp.max(near_scores, axis=-1, keepdims=True),
-            jnp.max(far_scores, axis=-1, keepdims=True),
-        )
-        near_weights = jnp.exp2(near_scores - top)
-        far_weights = jnp.exp2(far_scores - top)
-        total = jnp.sum(near_weights, axis=-1, keepdims=True) + jnp.sum(
-            far_weights, axis=-1, keepdims=True
-        )
-        mixed = weighted(near_weights, value[SPATIAL:, lanes]) + weighted(far_weights, far_values)
-        heads[:, lanes] = (mixed / total).astype(jnp.bfloat16)
-        return carry
-
-    lax.fori_loop(0, HEADS, attend, 0)
-
     row_frame = first_frame + lax.broadcasted_iota(jnp.int32, (ROWS, 1), 0) // SPATIAL
 
     def result_tile(j, carry):
@@ -481,7 +574,7 @@
     wires.drain()
 
 
-N_SLOTS = len(PIECES) * 16 + 1 + 2 * 9
+N_SLOTS = len(PIECES) * 16 + 1 + 2 * (1 + 4 * 8)
 
 
 def on_device(
@@ -522,6 +615,8 @@
             pltpu.VMEM((*gathered, 16, WIDTH), bf16),
             pltpu.VMEM((*gathered, 8, D), bf16),
             pltpu.VMEM((WIDTH, D), bf16),
+            pltpu.VMEM((EXT, WIDTH), jnp.float32),
+            pltpu.VMEM((EXT, WIDTH), jnp.float32),
             pltpu.VMEM((ROWS, WIDTH), bf16),
             pltpu.VMEM((EXT, WIDTH), bf16),
             pltpu.VMEM((EXT, WIDTH), bf16),
@@ -529,6 +624,9 @@
             pltpu.VMEM((4, 2, 4, MEM_DEV, WIDTH), bf16),
             pltpu.VMEM((HEADS, 2 * MEM_DEV, HD), jnp.float32),
             pltpu.VMEM((HEADS, 2 * MEM_DEV, HD), jnp.float32),
+            pltpu.VMEM((HEADS, ROWS, KEYS), bf16),
+            pltpu.VMEM((HEADS, ROWS, KEYS), bf16),
+            pltpu.VMEM((HEADS, ROWS, HD), jnp.float32),
             pltpu.VMEM((ROWS, WIDTH), bf16),
             pltpu.SemaphoreType.DMA((5,)),
             pltpu.SemaphoreType.DMA((N_SLOTS,)),
@@ -540,7 +638,7 @@
         name="memory_attention",
     )(
         video[0],
-        norm_gain.reshape(1, D),
+        norm_gain,
         query_weight,
         key_weight,
         value_weight,

time: 121 us -> 104 us (0.86)
  the two profiles are of different devices: /device:TPU:0 before, /device:TPU:1 now
where the time goes in v2:
time: 104 us; the launch traced here: 102 us
  Pallas kernels  99.7 us (96%)
  local copies, waits for them, and re-layouts  2.3 us (2%)
    pallas_call x1, Pallas kernels, on_device(): pl.pallas_call(body, out_shape=jax.ShapeDtypeStruct((ROWS, D), bf16), in_...  99.7 us
    unnamed x1, local copies, waits for them, and re-layouts  2.3 us

profile of v2, /device:TPU:1, one launch (start us, length us, event | category | flops | bytes accessed | tf_op | source)
XLA Modules:
  0.0 102.0 jit_solution(8463108810243597111)
XLA Ops:
  0.0 99.7 %memory_attention.1 = bf16[256,2048]{1,0:T(8,128)(2,1)} custom-call(bf16[256,2048]{1,0:T(8,128)(2,1)} %bitcast.3, bf16[2048]{0:T(1024)(128)(2,1)} %gain.1, bf16[16,1024]{1,0:T(8,128)(2,1)} %query_shard.1, bf16[16,1024]{1,0:T(8,128)(2,1)} %key_shard.1, bf16[16,1024]{1,0:T(8,128)(2,1)} %value_shard.1, bf16[27,1024]{1,0:T(8,128)(2,1)} %key_taps.1, ...), custom_call_target="tpu_custom_call" | custom-call | tf_op jit(solution)/shard_map/memory_attention/pallas_call | solution.py:595
  99.7 2.3 %copy.11 = bf16[1,256,2048]{2,1,0:T(8,128)(2,1)} copy(bf16[1,256,2048]{2,1,0:T(8,128)(2,1)} %bitcast.2) | data formatting | bytes 2097152

commit v3 on v2

--- a/solution.py
+++ b/solution.py
@@ -119,13 +119,12 @@
     ]
 
 
-class Ring:
+class Phase:
     def __init__(self, wires, view, place, core, axis, known, start, size, source=None):
-        self.wires, self.place, self.core, self.axis = wires, place, core, axis
+        self.wires, self.view, self.place, self.core = wires, view, place, core
+        self.axis, self.known, self.start, self.size = axis, known, start, size
         self.source = place if source is None else source
-        self.known, self.start, self.size = known, start, size
-        self.view = view
-        self.slots = [wires.slot() for _ in range(4)]
+        self.slots = [wires.slot() for _ in range(self.count)]
 
     def region(self, steps, start, size):
         place = {**moved(self.source, self.axis, steps), **{a: None for a in self.known}}
@@ -134,21 +133,48 @@
     def target(self, steps):
         return device(moved(self.place, self.axis, steps), self.core)
 
+    def send(self, number, steps, part, src=None, of=0):
+        region = self.region(of, *part)
+        src = region if src is None else src
+        self.wires.send(self.slots[number], src, region, self.target(steps))
+
+    def receive(self, number, steps, part, of):
+        self.wires.receive(self.slots[number], self.region(of, *part), self.target(-steps))
+
+
+class Direct(Phase):
+    count = 3
+
     def open(self, src=None):
-        mine = self.region(0, self.start, self.size)
-        for slot, steps in zip(self.slots[:2], (1, -1)):
-            self.wires.send(slot, mine if src is None else src, mine, self.target(steps))
+        for number, steps in enumerate((1, -1, 2)):
+            self.send(number, steps, (self.start, self.size), src)
+
+    def take(self, number):
+        steps = (1, -1, 2)[number]
+        self.receive(number, steps, (self.start, self.size), -steps)
+
+    def close(self):
+        for number in range(3):
+            self.take(number)
+
+
+class Ring(Phase):
+    count = 4
+
+    def open(self):
+        for number, steps in enumerate((1, -1)):
+            self.send(number, steps, (self.start, self.size))
 
     def relay(self):
-        for slot, steps, part in zip(self.slots[:2], (1, -1), halves(self.start, self.size)):
-            self.wires.receive(slot, self.region(-steps, self.start, self.size), self.target(-steps))
-        for slot, steps, part in zip(self.slots[2:], (1, -1), halves(self.start, self.size)):
-            region = self.region(-steps, *part)
-            self.wires.send(slot, region, region, self.target(steps))
+        parts = halves(self.start, self.size)
+        for number, steps in enumerate((1, -1)):
+            self.receive(number, steps, (self.start, self.size), -steps)
+            self.send(number + 2, steps, parts[number], of=-steps)
 
     def close(self):
-        for slot, steps, part in zip(self.slots[2:], (1, -1), halves(self.start, self.size)):
-            self.wires.receive(slot, self.region(2, *part), self.target(-steps))
+        parts = halves(self.start, self.size)
+        for number, steps in enumerate((1, -1)):
+            self.receive(number + 2, steps, parts[number], 2)
 
 
 class Gather:
@@ -157,34 +183,47 @@
         self.wires, self.ref, self.shard = wires, ref, shard
         self.place, self.core, self.order = place, core, order
         self.partner = device(place, 1 - core)
-        self.rings = [
-            Ring(
-                wires,
-                lambda at, start, size: weight_view(ref, core, at, start, size),
-                place,
-                core,
-                axis,
-                order[:k],
-                self.start,
-                self.size,
-            )
-            for k, axis in enumerate(order)
+        common = (
+            wires,
+            lambda at, start, size: weight_view(ref, core, at, start, size),
+            place,
+            core,
+        )
+        first, second, third = order
+        self.first = Direct(*common, first, "", self.start, self.size)
+        self.second = Direct(*common, second, first, self.start, self.size)
+        self.rows = [
+            Ring(*common, third, first, self.start, self.size, moved(place, second, steps))
+            for steps in (0, -1, 1, 2)
         ]
         self.slots = [wires.slot() for _ in range(4)]
 
     def open(self):
-        self.rings[0].open(self.shard.at[:, pl.ds(self.start, self.size)])
-
-    def relay(self, k):
-        self.rings[k].relay()
-
-    def close(self, k):
-        self.rings[k].close()
-        if k == 0:
-            self.rings[1].open()
+        self.first.open(self.shard.at[:, pl.ds(self.start, self.size)])
+
+    def spread(self, on=True):
+        self.first.close()
+        self.second.open()
+        if on:
+            self.rows[0].open()
+
+    def rise(self, on=True):
+        for number in range(3):
+            self.second.take(number)
+            if on:
+                self.rows[number + 1].open()
 
     def last(self):
-        self.rings[2].open()
+        for row in self.rows:
+            row.open()
+
+    def relay(self):
+        for row in self.rows:
+            row.relay()
+
+    def close(self):
+        for row in self.rows:
+            row.close()
 
     def region(self, core, steps):
         place = {
@@ -270,31 +309,15 @@
 
 class Memory:
     def __init__(self, wires, ref, place, core, order, start, own):
-        self.rings = [
-            Ring(
-                wires,
-                lambda at, first, size: memory_view(ref, at, first, size),
-                place,
-                core,
-                axis,
-                order[:k],
-                start,
-                HALF,
-                place if own else moved(place, "z", 2),
-            )
-            for k, axis in enumerate(order)
-        ]
-
-    def open(self):
-        self.rings[0].open()
-
-    def relay(self, k):
-        self.rings[k].relay()
-
-    def close(self, k):
-        self.rings[k].close()
-        if k == 0:
-            self.rings[1].open()
+        common = (
+            wires,
+            lambda at, first, size: memory_view(ref, at, first, size),
+            place,
+            core,
+        )
+        source = place if own else moved(place, "z", 2)
+        self.first = Direct(*common, order[0], "", start, HALF, source)
+        self.second = Ring(*common, order[1], order[0], start, HALF, source)
 
 
 def body(
@@ -324,8 +347,7 @@
     memory_value,
     spread_key,
     spread_value,
-    highs,
-    lows,
+    shares,
     totals,
     heads,
     local_sems,
@@ -345,7 +367,9 @@
 
     barrier = pltpu.get_barrier_semaphore()
     greeted = [device(moved(place, axis, steps), core) for axis in "xyz" for steps in (1, -1)]
+    greeted += [device(moved(place, axis, 2), core) for axis in "xyz"]
     greeted.append(partner)
+    greeted.append(device(moved(moved(place, "x", -1), "y", -1), core))
     for other in greeted:
         pl.semaphore_signal(barrier, inc=1, device_id=other, device_id_type=MESH)
 
@@ -395,38 +419,41 @@
         return carry
 
     lax.fori_loop(SPATIAL // 32, EXT // 32, normalize_at, 0)
-    for k in range(2):
-        for gather in everything:
-            gather.relay(k)
-        for gather in everything:
-            gather.close(k)
-            if k == 1 and gather in key_value:
-                gather.last()
+    for gather in key_value:
+        gather.spread()
 
     @pl.when(place["y"] == 3)
     def _():
         halo_copy.start()
 
     for gather in key_value:
+        gather.rise()
         gather.hand(0)
+
+    for number in range(4):
+        for gather in key_value:
+            gather.rows[number].relay()
+    for gather in query_part:
+        gather.spread()
+    for gather in out_part:
+        gather.spread(False)
     for gather in key_value:
-        gather.relay(2)
         gather.hand(1)
         gather.hand(2)
+    for gather in key_value:
+        gather.close()
+        gather.hand(3)
     for gather in query_part:
-        gather.last()
+        gather.rise()
         gather.hand(0)
     wires.receive(halo_slot, halo, (vid, before))
     lax.fori_loop(0, SPATIAL // 32, normalize_at, 0)
-    for gather in key_value:
-        gather.close(2)
-        gather.hand(3)
     project(normed, 0, EXT, key_w, core, key_partial, None)
     project(normed, 0, EXT, value_w, core, value_partial, None)
     for gather in key_value:
         gather.take()
     for gather in query_part:
-        gather.relay(2)
+        gather.relay()
         gather.hand(1)
         gather.hand(2)
     project(normed, 0, EXT, key_w, 1 - core, key_partial, key)
@@ -445,54 +472,63 @@
         pool(source, taps, valid, spread, ref, place)
         region = memory_view(ref, place, 0, WIDTH)
         slot = wires.slot()
-        parts = [
+        mine, other = (
             [
                 Memory(wires, ref, place, core, order, number * HALF, own_plane)
                 for number, order in enumerate(MEMORY_ORDERS)
             ]
             for own_plane in (True, False)
-        ]
-        for part in parts[0]:
-            part.open()
+        )
         wires.send(slot, region, region, across)
-        memories.append((ref, slot, parts))
+        for part in mine:
+            part.first.open()
+        memories.append((ref, slot, mine, other))
         if ref is memory_key:
             for gather in query_part:
-                gather.close(2)
+                gather.close()
                 gather.hand(3)
     for gather in out_part:
+        gather.rise(False)
         gather.last()
         gather.hand(0)
 
-    for ref, slot, (mine, other) in memories:
-        for part in mine:
-            part.relay(0)
-        wires.receive(slot, memory_view(ref, moved(place, "z", 2), 0, WIDTH), across)
-        for part in other:
-            part.open()
-        for part in mine:
-            part.close(0)
+    (key_ref, key_slot, key_mine, key_other), (value_ref, value_slot, value_mine, value_other) = memories
+    far_place = moved(place, "z", 2)
+    for part in key_mine:
+        part.first.close()
+        part.second.open()
+    wires.receive(key_slot, memory_view(key_ref, far_place, 0, WIDTH), across)
+    for part in key_other:
+        part.first.open()
+    for part in value_mine:
+        part.first.close()
+    wires.receive(value_slot, memory_view(value_ref, far_place, 0, WIDTH), across)
+    for part in value_other:
+        part.first.open()
+    for part in key_other:
+        part.first.close()
+        part.second.open()
+    for part in value_mine:
+        part.second.open()
+    for part in key_mine:
+        part.second.relay()
     for gather in query_part:
         gather.take()
     project(normed, SPATIAL, ROWS, query_w, core, key_partial, None)
-    for _, _, (mine, other) in memories:
-        for part in other:
-            part.relay(0)
-        for part in other:
-            part.close(0)
-    for _, _, (mine, other) in memories:
-        for part in mine:
-            part.relay(1)
+    for part in value_other:
+        part.first.close()
+        part.second.open()
+    for part in key_other:
+        part.second.relay()
+    project(normed, SPATIAL, ROWS, query_w, 1 - core, key_partial, query)
+    for part in value_mine:
+        part.second.relay()
     for gather in out_part:
-        gather.relay(2)
+        gather.relay()
         gather.hand(1)
         gather.hand(2)
-    project(normed, SPATIAL, ROWS, query_w, 1 - core, key_partial, query)
-    for _, _, (mine, other) in memories:
-        for part in other:
-            part.relay(1)
-    for part in memories[0][2][0] + memories[0][2][1]:
-        part.close(1)
+    for part in key_mine + key_other:
+        part.second.close()
 
     query_frame = lax.broadcasted_iota(jnp.int32, (ROWS, ROWS), 0) // SPATIAL
     key_frame = lax.broadcasted_iota(jnp.int32, (ROWS, ROWS), 1) // SPATIAL
@@ -516,37 +552,18 @@
         for first, scores in ((0, near_scores), (ROWS, far_scores)):
             exps = jnp.exp2(scores - top)
             total = total + jnp.sum(exps, axis=-1, keepdims=True)
-            high = exps.astype(jnp.bfloat16)
-            low = (exps - high.astype(jnp.float32)).astype(jnp.bfloat16)
-            highs[h, :, first : first + scores.shape[1]] = high
-            lows[h, :, first : first + scores.shape[1]] = low
+            shares[h, :, first : first + scores.shape[1]] = exps.astype(jnp.bfloat16)
         totals[h] = jnp.broadcast_to(total, (ROWS, HD))
         return carry
 
-    lax.fori_loop(0, HEADS, weigh, 0)
-
-    for part in memories[1][2][0] + memories[1][2][1]:
-        part.close(1)
+    lax.fori_loop(0, HEADS // 2, weigh, 0)
+    for part in value_other:
+        part.second.relay()
+    lax.fori_loop(HEADS // 2, HEADS, weigh, 0)
+
     for gather in out_part:
-        gather.close(2)
+        gather.close()
         gather.hand(3)
-
-    def mix(h, carry):
-        lanes = pl.ds(pl.multiple_of(h * HD, HD), HD)
-        near_values = value[SPATIAL:, lanes]
-        far_values = memory_value[:, :, :, :, lanes].reshape(N_TM * MEM_DEV, HD)
-        mixed = jnp.zeros((ROWS, HD), jnp.float32)
-        for part in (highs, lows):
-            mixed = mixed + jnp.dot(
-                part[h, :, :ROWS], near_values, preferred_element_type=jnp.float32
-            )
-            mixed = mixed + jnp.dot(
-                part[h, :, ROWS:], far_values, preferred_element_type=jnp.float32
-            )
-        heads[:, lanes] = (mixed / totals[h]).astype(jnp.bfloat16)
-        return carry
-
-    lax.fori_loop(0, HEADS, mix, 0)
     for gather in out_part:
         gather.take()
 
@@ -562,6 +579,21 @@
 
     lax.fori_loop(0, D // 256, out_tile, 0)
 
+    for part in value_mine + value_other:
+        part.second.close()
+
+    def mix(h, carry):
+        lanes = pl.ds(pl.multiple_of(h * HD, HD), HD)
+        near_values = value[SPATIAL:, lanes]
+        far_values = memory_value[:, :, :, :, lanes].reshape(N_TM * MEM_DEV, HD)
+        mixed = jnp.dot(shares[h, :, :ROWS], near_values, preferred_element_type=jnp.float32)
+        mixed = mixed + jnp.dot(
+            shares[h, :, ROWS:], far_values, preferred_element_type=jnp.float32
+        )
+        heads[:, lanes] = (mixed / totals[h]).astype(jnp.bfloat16)
+        return carry
+
+    lax.fori_loop(0, HEADS, mix, 0)
     row_frame = first_frame + lax.broadcasted_iota(jnp.int32, (ROWS, 1), 0) // SPATIAL
 
     def result_tile(j, carry):
@@ -574,7 +606,7 @@
     wires.drain()
 
 
-N_SLOTS = len(PIECES) * 16 + 1 + 2 * (1 + 4 * 8)
+N_SLOTS = len(PIECES) * 26 + 1 + 2 * (1 + 4 * 7)
 
 
 def on_device(
@@ -625,7 +657,6 @@
             pltpu.VMEM((HEADS, 2 * MEM_DEV, HD), jnp.float32),
             pltpu.VMEM((HEADS, 2 * MEM_DEV, HD), jnp.float32),
             pltpu.VMEM((HEADS, ROWS, KEYS), bf16),
-            pltpu.VMEM((HEADS, ROWS, KEYS), bf16),
             pltpu.VMEM((HEADS, ROWS, HD), jnp.float32),
             pltpu.VMEM((ROWS, WIDTH), bf16),
             pltpu.SemaphoreType.DMA((5,)),

time: 104 us -> 95.8 us (0.921); the launches traced: 102 us -> 95.6 us
  Pallas kernels: 99.7 us -> 93.3 us
    pallas_call x1, Pallas kernels: 99.7 us -> 93.3 us  [on_device(): pl.pallas_call(body, out_shape=jax.ShapeDtypeStruct((ROWS, D), bf16), in_...]
where the time goes in v3:
time: 95.8 us; the launch traced here: 95.6 us
  Pallas kernels  93.3 us (97%)
  local copies, waits for them, and re-layouts  2.3 us (2%)
    pallas_call x1, Pallas kernels, on_device(): pl.pallas_call(body, out_shape=jax.ShapeDtypeStruct((ROWS, D), bf16), in_...  93.3 us
    unnamed x1, local copies, waits for them, and re-layouts  2.3 us

profile of v3, /device:TPU:1, one launch (start us, length us, event | category | flops | bytes accessed | tf_op | source)
XLA Modules:
  0.0 95.6 jit_solution(5980062348587601238)
XLA Ops:
  0.0 93.3 %memory_attention.1 = bf16[256,2048]{1,0:T(8,128)(2,1)} custom-call(bf16[256,2048]{1,0:T(8,128)(2,1)} %bitcast.3, bf16[2048]{0:T(1024)(128)(2,1)} %gain.1, bf16[16,1024]{1,0:T(8,128)(2,1)} %query_shard.1, bf16[16,1024]{1,0:T(8,128)(2,1)} %key_shard.1, bf16[16,1024]{1,0:T(8,128)(2,1)} %value_shard.1, bf16[27,1024]{1,0:T(8,128)(2,1)} %key_taps.1, ...), custom_call_target="tpu_custom_call" | custom-call | tf_op jit(solution)/shard_map/memory_attention/pallas_call | solution.py:627
  93.3 2.3 %copy.11 = bf16[1,256,2048]{2,1,0:T(8,128)(2,1)} copy(bf16[1,256,2048]{2,1,0:T(8,128)(2,1)} %bitcast.2) | data formatting | bytes 2097152

commit v4 on v3

--- a/solution.py
+++ b/solution.py
@@ -556,10 +556,10 @@
         totals[h] = jnp.broadcast_to(total, (ROWS, HD))
         return carry
 
-    lax.fori_loop(0, HEADS // 2, weigh, 0)
+    lax.fori_loop(0, HEADS // 2, weigh, 0, unroll=2)
     for part in value_other:
         part.second.relay()
-    lax.fori_loop(HEADS // 2, HEADS, weigh, 0)
+    lax.fori_loop(HEADS // 2, HEADS, weigh, 0, unroll=2)
 
     for gather in out_part:
         gather.close()
@@ -593,16 +593,16 @@
         heads[:, lanes] = (mixed / totals[h]).astype(jnp.bfloat16)
         return carry
 
-    lax.fori_loop(0, HEADS, mix, 0)
+    lax.fori_loop(0, HEADS, mix, 0, unroll=4)
     row_frame = first_frame + lax.broadcasted_iota(jnp.int32, (ROWS, 1), 0) // SPATIAL
 
     def result_tile(j, carry):
-        columns = pl.ds(pl.multiple_of(j * 256, 256), 256)
+        columns = pl.ds(pl.multiple_of(j * 512, 512), 512)
         result = jnp.dot(heads[...], out_rows[:, columns], preferred_element_type=jnp.float32)
         out[:, columns] = jnp.where(row_frame < limit, result, 0.0).astype(jnp.bfloat16)
         return carry
 
-    lax.fori_loop(0, D // 256, result_tile, 0)
+    lax.fori_loop(0, D // 512, result_tile, 0, unroll=2)
     wires.drain()
 
 

time: 95.8 us -> 92.4 us (0.965)
  Pallas kernels: 93.3 us -> 89.9 us
    pallas_call x1, Pallas kernels: 93.3 us -> 89.9 us  [on_device(): pl.pallas_call(body, out_shape=jax.ShapeDtypeStruct((ROWS, D), bf16), in_...]
where the time goes in v4:
time: 92.4 us; the launch traced here: 92.2 us
  Pallas kernels  89.9 us (97%)
  local copies, waits for them, and re-layouts  2.3 us (2%)
    pallas_call x1, Pallas kernels, on_device(): pl.pallas_call(body, out_shape=jax.ShapeDtypeStruct((ROWS, D), bf16), in_...  89.9 us
    unnamed x1, local copies, waits for them, and re-layouts  2.3 us

profile of v4, /device:TPU:1, one launch (start us, length us, event | category | flops | bytes accessed | tf_op | source)
XLA Modules:
  0.0 92.2 jit_solution(1914810405194358697)
XLA Ops:
  0.0 89.9 %memory_attention.1 = bf16[256,2048]{1,0:T(8,128)(2,1)} custom-call(bf16[256,2048]{1,0:T(8,128)(2,1)} %bitcast.3, bf16[2048]{0:T(1024)(128)(2,1)} %gain.1, bf16[16,1024]{1,0:T(8,128)(2,1)} %query_shard.1, bf16[16,1024]{1,0:T(8,128)(2,1)} %key_shard.1, bf16[16,1024]{1,0:T(8,128)(2,1)} %value_shard.1, bf16[27,1024]{1,0:T(8,128)(2,1)} %key_taps.1, ...), custom_call_target="tpu_custom_call" | custom-call | tf_op jit(solution)/shard_map/memory_attention/pallas_call | solution.py:627
  89.9 2.3 %copy.11 = bf16[1,256,2048]{2,1,0:T(8,128)(2,1)} copy(bf16[1,256,2048]{2,1,0:T(8,128)(2,1)} %bitcast.2) | data formatting | bytes 2097152

commit v5 on v4

--- a/solution.py
+++ b/solution.py
@@ -48,7 +48,6 @@
 
 def halves(start, size):
     first = (size // 256) * 128 if size > 128 else size
-    first = size - first
     return ((start, first), (start + first, size - first))
 
 
@@ -264,7 +263,7 @@
             out[:, columns] = total.astype(jnp.bfloat16)
         return carry
 
-    lax.fori_loop(0, WIDTH // 256, tile, 0)
+    lax.fori_loop(0, WIDTH // 256, tile, 0, unroll=2)
 
 
 def pool(source, taps, valid, spread_tmp, out, place):
@@ -298,7 +297,7 @@
         out[place["x"], place["z"] // 2, place["y"], :, lanes] = normed.astype(jnp.bfloat16)
         return carry
 
-    lax.fori_loop(0, HEADS, head, 0)
+    lax.fori_loop(0, HEADS, head, 0, unroll=2)
 
 
 def scores_of(queries, keys):

time: 92.4 us -> 89.8 us (0.972)
  Pallas kernels: 89.9 us -> 87.3 us
    pallas_call x1, Pallas kernels: 89.9 us -> 87.3 us  [on_device(): pl.pallas_call(body, out_shape=jax.ShapeDtypeStruct((ROWS, D), bf16), in_...]
where the time goes in v5:
time: 89.8 us; the launch traced here: 89.6 us
  Pallas kernels  87.3 us (97%)
  local copies, waits for them, and re-layouts  2.3 us (3%)
    pallas_call x1, Pallas kernels, on_device(): pl.pallas_call(body, out_shape=jax.ShapeDtypeStruct((ROWS, D), bf16), in_...  87.3 us
    unnamed x1, local copies, waits for them, and re-layouts  2.3 us

profile of v5, /device:TPU:1, one launch (start us, length us, event | category | flops | bytes accessed | tf_op | source)
XLA Modules:
  0.0 89.6 jit_solution(6600943936108114969)
XLA Ops:
  0.0 87.3 %memory_attention.1 = bf16[256,2048]{1,0:T(8,128)(2,1)} custom-call(bf16[256,2048]{1,0:T(8,128)(2,1)} %bitcast.3, bf16[2048]{0:T(1024)(128)(2,1)} %gain.1, bf16[16,1024]{1,0:T(8,128)(2,1)} %query_shard.1, bf16[16,1024]{1,0:T(8,128)(2,1)} %key_shard.1, bf16[16,1024]{1,0:T(8,128)(2,1)} %value_shard.1, bf16[27,1024]{1,0:T(8,128)(2,1)} %key_taps.1, ...), custom_call_target="tpu_custom_call" | custom-call | tf_op jit(solution)/shard_map/memory_attention/pallas_call | solution.py:626
  87.3 2.3 %copy.11 = bf16[1,256,2048]{2,1,0:T(8,128)(2,1)} copy(bf16[1,256,2048]{2,1,0:T(8,128)(2,1)} %bitcast.2) | data formatting | bytes 2097152

commit v6 on v5

--- a/solution.py
+++ b/solution.py
@@ -263,7 +263,7 @@
             out[:, columns] = total.astype(jnp.bfloat16)
         return carry
 
-    lax.fori_loop(0, WIDTH // 256, tile, 0, unroll=2)
+    lax.fori_loop(0, WIDTH // 256, tile, 0, unroll=4)
 
 
 def pool(source, taps, valid, spread_tmp, out, place):
@@ -297,7 +297,7 @@
         out[place["x"], place["z"] // 2, place["y"], :, lanes] = normed.astype(jnp.bfloat16)
         return carry
 
-    lax.fori_loop(0, HEADS, head, 0, unroll=2)
+    lax.fori_loop(0, HEADS, head, 0, unroll=4)
 
 
 def scores_of(queries, keys):
@@ -555,10 +555,10 @@
         totals[h] = jnp.broadcast_to(total, (ROWS, HD))
         return carry
 
-    lax.fori_loop(0, HEADS // 2, weigh, 0, unroll=2)
+    lax.fori_loop(0, HEADS // 2, weigh, 0, unroll=4)
     for part in value_other:
         part.second.relay()
-    lax.fori_loop(HEADS // 2, HEADS, weigh, 0, unroll=2)
+    lax.fori_loop(HEADS // 2, HEADS, weigh, 0, unroll=4)
 
     for gather in out_part:
         gather.close()
@@ -576,7 +576,7 @@
         )
         return carry
 
-    lax.fori_loop(0, D // 256, out_tile, 0)
+    lax.fori_loop(0, D // 256, out_tile, 0, unroll=4)
 
     for part in value_mine + value_other:
         part.second.close()
@@ -592,7 +592,7 @@
         heads[:, lanes] = (mixed / totals[h]).astype(jnp.bfloat16)
         return carry
 
-    lax.fori_loop(0, HEADS, mix, 0, unroll=4)
+    lax.fori_loop(0, HEADS, mix, 0, unroll=8)
     row_frame = first_frame + lax.broadcasted_iota(jnp.int32, (ROWS, 1), 0) // SPATIAL
 
     def result_tile(j, carry):
@@ -601,7 +601,7 @@
         out[:, columns] = jnp.where(row_frame < limit, result, 0.0).astype(jnp.bfloat16)
         return carry
 
-    lax.fori_loop(0, D // 512, result_tile, 0, unroll=2)
+    lax.fori_loop(0, D // 512, result_tile, 0, unroll=4)
     wires.drain()
 
 

time: 89.8 us -> 87.9 us (0.979)
  Pallas kernels: 87.3 us -> 85.4 us
    pallas_call x1, Pallas kernels: 87.3 us -> 85.4 us  [on_device(): pl.pallas_call(body, out_shape=jax.ShapeDtypeStruct((ROWS, D), bf16), in_...]
where the time goes in v6:
time: 87.9 us; the launch traced here: 87.7 us
  Pallas kernels  85.4 us (97%)
  local copies, waits for them, and re-layouts  2.3 us (3%)
    pallas_call x1, Pallas kernels, on_device(): pl.pallas_call(body, out_shape=jax.ShapeDtypeStruct((ROWS, D), bf16), in_...  85.4 us
    unnamed x1, local copies, waits for them, and re-layouts  2.3 us

profile of v6, /device:TPU:1, one launch (start us, length us, event | category | flops | bytes accessed | tf_op | source)
XLA Modules:
  0.0 87.7 jit_solution(6254543073400477204)
XLA Ops:
  0.0 85.4 %memory_attention.1 = bf16[256,2048]{1,0:T(8,128)(2,1)} custom-call(bf16[256,2048]{1,0:T(8,128)(2,1)} %bitcast.3, bf16[2048]{0:T(1024)(128)(2,1)} %gain.1, bf16[16,1024]{1,0:T(8,128)(2,1)} %query_shard.1, bf16[16,1024]{1,0:T(8,128)(2,1)} %key_shard.1, bf16[16,1024]{1,0:T(8,128)(2,1)} %value_shard.1, bf16[27,1024]{1,0:T(8,128)(2,1)} %key_taps.1, ...), custom_call_target="tpu_custom_call" | custom-call | tf_op jit(solution)/shard_map/memory_attention/pallas_call | solution.py:626
  85.4 2.3 %copy.11 = bf16[1,256,2048]{2,1,0:T(8,128)(2,1)} copy(bf16[1,256,2048]{2,1,0:T(8,128)(2,1)} %bitcast.2) | data formatting | bytes 2097152
